TPU v7x, 32 devices: a whole 2x2x4 slice. The times are simulated.
32 devices in a mesh: blk: 8 (over z, y), plane: 4 (over x, core).
Axes of the slice: x: 2, y: 2, z: 4, core: 2. Of those that a mesh axis runs over, the one named last changes fastest.
Arguments:
- tiles: bfloat16 [128, 24, 128, 128], P(('blk', 'plane')), may hold values from -0.25 to 0.25
- tile_cols: int32 [128, 24], P(('blk', 'plane')), may hold values from 0 to 511
- tile_count: int32 [128], P(('blk', 'plane')), may hold values from 18 to 24, as said below
- u_start: float32 [16384], P(('blk', 'plane')), may hold values from -0.046875 to 0.046875
- v_start: float32 [65536], P(('blk', 'plane')), may hold values from -0.0234375 to 0.0234375
- beta_start: float32 [1], replicated, may hold values from 0.5 to 1.5
- left_basis: float32 [16384, 128], P(('blk', 'plane')), may hold values from -0.046875 to 0.046875
- right_basis: float32 [65536, 128], P(('blk', 'plane')), may hold values from -0.0234375 to 0.0234375
Outputs:
- left_vectors: float32 [1, 16384], P(None, ('blk', 'plane'))
- right_vectors: float32 [1, 65536], P(None, ('blk', 'plane'))
- coefficients: float32 [2], replicated
Inputs may be any that keep to these rules, and one draw needn't show every extreme that they name: `tile_count`: slots at and after a row block's count are padding; some row block uses all 24 slots.
All inputs are finite; a program needn't handle non-finite values.
Results may differ from a plain program's by a relative error of at most 0.00055.
The roundings to bfloat16 on the way count: a program that leaves them out, or rounds other values in their place, can miss the bound.
Values may be sent and summed in bfloat16 or wider, within the bound.
No kernel may reach another device: no remote copies, remote signals or barrier semaphores. Data moves between devices by JAX's collectives and lax.ppermute only.
A program may use at most 64 MiB of HBM per device.

v0:
```python
import math
import jax
import jax.numpy as jnp
from jax import lax
from jax.sharding import PartitionSpec as P


def project_twice(vec, basis, gram):
    high = lax.Precision.HIGHEST
    first, whole_sq = lax.psum(
        (jnp.dot(vec, basis, precision=high), jnp.sum(vec * vec)), ("blk", "plane")
    )
    coef = 2.0 * first - jnp.dot(gram, first, precision=high)
    vec = vec - jnp.dot(basis, coef, precision=high)
    total = (
        whole_sq - 2.0 * jnp.sum(coef * first) + jnp.sum(coef * jnp.dot(gram, coef, precision=high))
    )
    norm = jnp.sqrt(total + 1e-06)
    return (vec / norm, norm)


def on_device(tiles, tile_cols, tile_count, u_start, v_start, beta_start, left_basis, right_basis):
    high = lax.Precision.HIGHEST
    devices = lax.axis_size(("blk", "plane"))
    blocks, slots = tile_cols.shape
    n_tiles = v_start.shape[0] * devices // 128
    live = (lax.iota(jnp.int32, slots)[None, :] < tile_count[:, None]).astype(jnp.float32)
    onehot = (tile_cols.reshape(-1)[:, None] == lax.iota(jnp.int32, n_tiles)[None, :]).astype(
        jnp.float32
    )
    left_gram, right_gram = lax.psum(
        (
            jnp.dot(left_basis.T, left_basis, precision=high),
            jnp.dot(right_basis.T, right_basis, precision=high),
        ),
        ("blk", "plane"),
    )
    left_scale = math.sqrt(u_start.shape[0] * devices)
    right_scale = math.sqrt(v_start.shape[0] * devices)
    vec_right = v_start
    vec_left = u_start
    beta = beta_start[0]
    lefts, rights, coefs = ([], [], [])
    rounded = vec_right.astype(jnp.bfloat16)
    whole = lax.all_gather(rounded, ("blk", "plane"), axis=0, tiled=True)
    table = whole.reshape(n_tiles, 128)
    picked = jnp.take(table, tile_cols, axis=0)
    values = jnp.einsum("rsij,rsj->rsi", tiles, picked, preferred_element_type=jnp.float32)
    forward_out = jnp.sum(values * live[:, :, None], axis=1).reshape(-1)
    vec_left, alpha = project_twice(forward_out - beta * vec_left, left_basis, left_gram)
    left_rows = vec_left.astype(jnp.bfloat16).reshape(blocks, 128)
    contrib = jnp.einsum("rsij,ri->rsj", tiles, left_rows, preferred_element_type=jnp.float32)
    contrib = (contrib * live[:, :, None]).reshape(-1, 128)
    partial_value = lax.dot_general(onehot, contrib, (((0,), (0,)), ((), ())), precision=high)
    owned = lax.psum_scatter(partial_value, ("blk", "plane"), scatter_dimension=0, tiled=True)
    back_out = owned.reshape(-1)
    vec_right, beta = project_twice(back_out - alpha * vec_right, right_basis, right_gram)
    lefts.append(vec_left * left_scale)
    rights.append(vec_right * right_scale)
    coefs.append(alpha)
    coefs.append(beta)
    return (jnp.stack(lefts), jnp.stack(rights), jnp.stack(coefs))


def solution(mesh):
    placed = (
        P(("blk", "plane"), None, None, None),
        P(("blk", "plane"), None),
        P(("blk", "plane")),
        P(("blk", "plane")),
        P(("blk", "plane")),
        P(),
        P(("blk", "plane"), None),
        P(("blk", "plane"), None),
    )
    return jax.shard_map(
        on_device,
        mesh=mesh,
        in_specs=placed,
        out_specs=(P(None, ("blk", "plane")), P(None, ("blk", "plane")), P()),
        check_vma=False,
    )
```

profile of v0, /device:TPU:12, one launch (start us, length us, event | category | flops | bytes accessed | tf_op | source)
XLA Modules:
  0.0 338.8 jit_solution(10103056694969738724)
XLA Ops:
  7.2 2.4 fusion.21
  9.6 4.1 %fusion.22 = f32[128,128]{1,0:T(8,128)} fusion(f32[2048,128]{1,0:T(8,128)} %param.15), kind=kOutput, calls=%fused_computation.48 | convolution fusion | flops 402653184 | bytes 1114112 | tf_op jit(solution)/shard_map/dot_general | solution.py:34
  13.8 0.7 compare_and_fusion
  14.5 0.8 eq.15
  15.2 0.7 compare_select_fusion
  16.6 0.7 fusion.12
  17.4 0.7 convert_element_type.14
  18.1 32.0 %all_gather.3 = bf16[65536]{0:T(1024)(128)(2,1)S(1)} all-gather(bf16[2048]{0:T(1024)(128)(2,1)S(1)} %convert_element_type.14), channel_id=1, replica_groups=mesh['blk'=8,'plane'=4] {'blk','plane'}, dimensions={0}, use_global_device_ids=true | all-gather | bytes 135168 | tf_op jit(solution)/shard_map/all_gather | solution.py:45
  50.1 1.3 gather_fusion
  51.4 0.8 select_bitcast_fusion
  52.3 1.7 fusion.8
  54.1 1.3 multiply_reduce_fusion.2
  55.6 49.4 %all-reduce.1 = (f32[128]{0:T(128)S(1)}, f32[]{:T(128)}) all-reduce(f32[128]{0:T(128)S(1)} %convolution_bitcast_fusion.1, f32[]{:T(128)} %get-tuple-element.13), channel_id=1, replica_groups=mesh['blk'=8,'plane'=4] {'blk','plane'}, use_global_device_ids=true, to_apply=%region_1.0 | all-reduce | flops 129 | bytes 1032 | tf_op jit(solution)/shard_map/psum | solution.py:10
  105.0 34.8 %all-reduce.5.cloned.1.call-done = (f32[128,128]{1,0:T(8,128)}, f32[128,128]{1,0:T(8,128)}) async-done(((f32[128,128]{1,0:T(8,128)}, f32[128,128]{1,0:T(8,128)}), (f32[128,128]{1,0:T(8,128)}, f32[128,128]{1,0:T(8,128)})) %all-reduce.5.cloned.1.call-update) | async-done | bytes 131088 | tf_op jit(solution)/shard_map/psum | solution.py:31
  139.8 1.7 multiply_reduce_fusion.4
  141.5 1.7 fusion.4
  146.1 1.2 fusion.6
  147.9 106.2 %reduce-scatter.2.cloned.1.call-done = f32[16,128]{1,0:T(8,128)} async-done(((f32[512,128]{1,0:T(8,128)}), f32[16,128]{1,0:T(8,128)}) %reduce-scatter.2.cloned.1.call-update) | async-done | bytes 8208 | tf_op jit(solution)/shard_map/reduce_scatter | solution.py:55
  254.1 1.3 multiply_reduce_fusion.1
  255.4 1.8 convolution_bitcast_fusion
  257.2 67.5 %all-reduce = (f32[128]{0:T(128)S(1)}, f32[]{:T(128)}) all-reduce(f32[128]{0:T(128)S(1)} %convolution_bitcast_fusion, f32[]{:T(128)} %get-tuple-element.9), channel_id=1, replica_groups=mesh['blk'=8,'plane'=4] {'blk','plane'}, use_global_device_ids=true, to_apply=%region_8.9 | all-reduce | flops 129 | bytes 1032 | tf_op jit(solution)/shard_map/psum | solution.py:10
  324.8 0.8 multiply_reduce_fusion.3
  325.6 0.9 fusion.5
  326.5 2.2 fusion.14
  (23 shorter events, 3.2 us)
Async XLA Ops:
  7.2 45.1 %copy-start = (bf16[4,24,128,128]{3,2,1,0:T(8,128)(2,1)S(1)}, bf16[4,24,128,128]{3,2,1,0:T(8,128)(2,1)}, u32[]{:S(2)}) copy-start(bf16[4,24,128,128]{3,2,1,0:T(8,128)(2,1)} %param.8) | copy-start | bytes 9437188
  7.2 132.6 %all-reduce.5.cloned.1.call-start = ((), (), s32[]{:S(2)}) async-start(), calls=%async_computation.2 | async-start | bytes 262144 | tf_op jit(solution)/shard_map/psum | solution.py:31
  9.6 45.8 %copy-start.1 = (f32[512,128]{1,0:T(8,128)S(1)}, f32[512,128]{1,0:T(8,128)}, u32[]{:S(2)}) copy-start(f32[512,128]{1,0:T(8,128)} %param.14) | copy-start | bytes 786436
  13.7 240.3 %reduce-scatter.2.cloned.1.call-start = ((), (), s32[]{:S(2)}) async-start(), calls=%async_computation.1 | async-start | bytes 270336 | tf_op jit(solution)/shard_map/reduce_scatter | solution.py:55
  52.2 201.9 %copy-start.3 = (f32[2048]{0:T(1024)S(1)}, f32[2048]{0:T(1024)}, u32[]{:S(2)}) copy-start(f32[2048]{0:T(1024)} %param.12) | copy-start | bytes 24580
  139.8 185.0 %copy-start.2 = (f32[128,128]{1,0:T(8,128)S(1)}, f32[128,128]{1,0:T(8,128)}, u32[]{:S(2)}) copy-start(f32[128,128]{1,0:T(8,128)} %get-tuple-element.8) | copy-start | bytes 196612
Sparse Core Ops, SparseCore 0:
  13.9 125.9 all-reduce.4
  147.4 106.6 reduce-scatter.1
where the time goes:
time: 340 us; the launch traced here: 339 us
  blocking collectives  149 us (44%)
  waiting for transfers between devices  141 us (41%)
  matrix products  19.5 us (6%)
  between operations  18.8 us (6%)
  other arithmetic  8.19 us (2%)
    psum x2, blocking collectives, project_twice(): lax.psum((jnp.dot(vec, basis, precision=high), jnp.sum(vec * vec)), ('blk...  117 us
    reduce_scatter x1, waiting for transfers between devices, on_device(): lax.psum_scatter(partial_value, ('blk', 'plane'), scatter_dimension=0, ti...  106 us
    psum x1, waiting for transfers between devices, on_device(): lax.psum((jnp.dot(left_basis.T, left_basis, precision=high), jnp.dot(righ...  34.8 us
    all_gather x1, blocking collectives, on_device(): whole = lax.all_gather(rounded, ('blk', 'plane'), axis=0, tiled=True)  32 us
  transfers between devices with their start and end apart: 2, of which 2 were waited for; matrix products, arithmetic and copies ran while one was open for 3% of the time, Pallas kernels for 0%

commit v1 on v0

--- a/solution.py
+++ b/solution.py
@@ -5,10 +5,15 @@
 from jax.sharding import PartitionSpec as P
 
 
+def one_after_other(value, leading, second):
+    partial = lax.psum(value, leading)
+    return lax.psum(partial, second)
+
+
 def project_twice(vec, basis, gram):
     high = lax.Precision.HIGHEST
-    first, whole_sq = lax.psum(
-        (jnp.dot(vec, basis, precision=high), jnp.sum(vec * vec)), ("blk", "plane")
+    first, whole_sq = one_after_other(
+        (jnp.dot(vec, basis, precision=high), jnp.sum(vec * vec)), "plane", "blk"
     )
     coef = 2.0 * first - jnp.dot(gram, first, precision=high)
     vec = vec - jnp.dot(basis, coef, precision=high)

time: 340 us -> 326 us (0.959); the launches traced: 339 us -> 321 us
  blocking collectives: 149 us -> 114 us
  waiting for transfers between devices: 141 us -> 158 us
    psum x2 -> x4, blocking collectives: 117 us -> 82.2 us  [the longest x2 69.2 us: one_after_other(): return lax.psum(partial, second)]
    psum x1, waiting for transfers between devices: 34.8 us -> 52.1 us  [on_device(): lax.psum((jnp.dot(left_basis.T, left_basis, precision=high), jnp.dot(righ...]
where the time goes in v1:
time: 326 us; the launch traced here: 321 us
  waiting for transfers between devices  158 us (48%)
  blocking collectives  114 us (35%)
  matrix products  19.5 us (6%)
  between operations  18.8 us (6%)
  other arithmetic  8.19 us (3%)
    reduce_scatter x1, waiting for transfers between devices, on_device(): lax.psum_scatter(partial_value, ('blk', 'plane'), scatter_dimension=0, ti...  106 us
    psum x2, blocking collectives, one_after_other(): return lax.psum(partial, second)  69.2 us
    psum x1, waiting for transfers between devices, on_device(): lax.psum((jnp.dot(left_basis.T, left_basis, precision=high), jnp.dot(righ...  52.1 us
    all_gather x1, blocking collectives, on_device(): whole = lax.all_gather(rounded, ('blk', 'plane'), axis=0, tiled=True)  32 us
    psum x2, blocking collectives, one_after_other(): partial = lax.psum(value, leading)  13 us
  transfers between devices with their start and end apart: 2, of which 2 were waited for; matrix products, arithmetic and copies ran while one was open for 3% of the time, Pallas kernels for 0%

profile of v1, /device:TPU:12, one launch (start us, length us, event | category | flops | bytes accessed | tf_op | source)
XLA Modules:
  0.0 321.2 jit_solution(8883117752325938917)
XLA Ops:
  7.2 2.4 fusion.21
  9.6 4.1 %fusion.22 = f32[128,128]{1,0:T(8,128)} fusion(f32[2048,128]{1,0:T(8,128)} %param.15), kind=kOutput, calls=%fused_computation.48 | convolution fusion | flops 402653184 | bytes 1114112 | tf_op jit(solution)/shard_map/dot_general | solution.py:39
  14.5 0.8 eq.15
  16.6 0.7 fusion.12
  17.4 0.7 convert_element_type.14
  18.1 32.0 %all_gather.3 = bf16[65536]{0:T(1024)(128)(2,1)S(1)} all-gather(bf16[2048]{0:T(1024)(128)(2,1)S(1)} %convert_element_type.14), channel_id=1, replica_groups=mesh['blk'=8,'plane'=4] {'blk','plane'}, dimensions={0}, use_global_device_ids=true | all-gather | bytes 135168 | tf_op jit(solution)/shard_map/all_gather | solution.py:50
  50.1 1.3 gather_fusion
  51.4 0.8 select_bitcast_fusion
  52.3 1.7 fusion.8
  54.1 1.3 multiply_reduce_fusion.2
  55.6 6.6 %all-reduce.4 = (f32[128]{0:T(128)S(1)}, f32[]{:T(128)}) all-reduce(f32[128]{0:T(128)S(1)} %convolution_bitcast_fusion.1, f32[]{:T(128)} %get-tuple-element.17), channel_id=1, replica_groups=mesh['blk'=8,'plane'=4] {'plane'}, use_global_device_ids=true, to_apply=%region_1.0 | all-reduce | flops 129 | bytes 1032 | tf_op jit(solution)/shard_map/psum | solution.py:9
  62.2 25.5 %all-reduce.2 = (f32[128]{0:T(128)S(1)}, f32[]{:T(128)}) all-reduce(f32[128]{0:T(128)S(1)} %get-tuple-element.11, f32[]{:T(128)} %get-tuple-element.12), channel_id=1, replica_groups=mesh['blk'=8,'plane'=4] {'blk'}, use_global_device_ids=true, to_apply=%region_2.3 | all-reduce | flops 129 | bytes 1032 | tf_op jit(solution)/shard_map/psum | solution.py:10
  87.7 52.1 %all-reduce.7.cloned.1.call-done = (f32[128,128]{1,0:T(8,128)}, f32[128,128]{1,0:T(8,128)}) async-done(((f32[128,128]{1,0:T(8,128)}, f32[128,128]{1,0:T(8,128)}), (f32[128,128]{1,0:T(8,128)}, f32[128,128]{1,0:T(8,128)})) %all-reduce.7.cloned.1.call-update) | async-done | bytes 131088 | tf_op jit(solution)/shard_map/psum | solution.py:36
  139.8 1.7 multiply_reduce_fusion.4
  141.5 1.7 fusion.4
  146.1 1.2 fusion.6
  147.9 106.2 %reduce-scatter.2.cloned.1.call-done = f32[16,128]{1,0:T(8,128)} async-done(((f32[512,128]{1,0:T(8,128)}), f32[16,128]{1,0:T(8,128)}) %reduce-scatter.2.cloned.1.call-update) | async-done | bytes 8208 | tf_op jit(solution)/shard_map/reduce_scatter | solution.py:60
  254.1 1.3 multiply_reduce_fusion.1
  255.4 1.8 convolution_bitcast_fusion
  257.2 6.4 %all-reduce.3 = (f32[128]{0:T(128)S(1)}, f32[]{:T(128)}) all-reduce(f32[128]{0:T(128)S(1)} %convolution_bitcast_fusion, f32[]{:T(128)} %get-tuple-element.13), channel_id=1, replica_groups=mesh['blk'=8,'plane'=4] {'plane'}, use_global_device_ids=true, to_apply=%region_10.11 | all-reduce | flops 129 | bytes 1032 | tf_op jit(solution)/shard_map/psum | solution.py:9
  263.6 43.7 %all-reduce.1 = (f32[128]{0:T(128)S(1)}, f32[]{:T(128)}) all-reduce(f32[128]{0:T(128)S(1)} %get-tuple-element.9, f32[]{:T(128)} %get-tuple-element.10), channel_id=1, replica_groups=mesh['blk'=8,'plane'=4] {'blk'}, use_global_device_ids=true, to_apply=%region_11.12 | all-reduce | flops 129 | bytes 1032 | tf_op jit(solution)/shard_map/psum | solution.py:10
  307.3 0.8 multiply_reduce_fusion.3
  308.1 0.9 fusion.5
  309.0 2.2 fusion.14
  (25 shorter events, 4.6 us)
Async XLA Ops:
  7.2 45.1 %copy-start = (bf16[4,24,128,128]{3,2,1,0:T(8,128)(2,1)S(1)}, bf16[4,24,128,128]{3,2,1,0:T(8,128)(2,1)}, u32[]{:S(2)}) copy-start(bf16[4,24,128,128]{3,2,1,0:T(8,128)(2,1)} %param.8) | copy-start | bytes 9437188
  7.2 132.6 %all-reduce.7.cloned.1.call-start = ((), (), s32[]{:S(2)}) async-start(), calls=%async_computation.2 | async-start | bytes 262144 | tf_op jit(solution)/shard_map/psum | solution.py:36
  9.6 45.8 %copy-start.1 = (f32[512,128]{1,0:T(8,128)S(1)}, f32[512,128]{1,0:T(8,128)}, u32[]{:S(2)}) copy-start(f32[512,128]{1,0:T(8,128)} %param.14) | copy-start | bytes 786436
  13.7 240.3 %reduce-scatter.2.cloned.1.call-start = ((), (), s32[]{:S(2)}) async-start(), calls=%async_computation.1 | async-start | bytes 270336 | tf_op jit(solution)/shard_map/reduce_scatter | solution.py:60
  52.2 201.8 %copy-start.3 = (f32[2048]{0:T(1024)S(1)}, f32[2048]{0:T(1024)}, u32[]{:S(2)}) copy-start(f32[2048]{0:T(1024)} %param.12) | copy-start | bytes 24580
  139.8 167.5 %copy-start.2 = (f32[128,128]{1,0:T(8,128)S(1)}, f32[128,128]{1,0:T(8,128)}, u32[]{:S(2)}) copy-start(f32[128,128]{1,0:T(8,128)} %get-tuple-element.4) | copy-start | bytes 196612
Sparse Core Ops, SparseCore 0:
  13.9 125.8 all-reduce.6
  147.4 106.6 reduce-scatter.1

commit v2 on v0

--- a/solution.py
+++ b/solution.py
@@ -1,8 +1,17 @@
+import functools
 import math
 import jax
 import jax.numpy as jnp
 from jax import lax
 from jax.sharding import PartitionSpec as P
+
+
+def _convert_stacks_all(view, along_axis, device_axis):
+    last = jax.lax.psum(view, along_axis)
+    return jax.lax.psum(last, device_axis)
+
+
+slabs_register = functools.partial(_convert_stacks_all, along_axis="blk", device_axis="plane")
 
 
 def project_twice(vec, basis, gram):
@@ -28,12 +37,11 @@
     onehot = (tile_cols.reshape(-1)[:, None] == lax.iota(jnp.int32, n_tiles)[None, :]).astype(
         jnp.float32
     )
-    left_gram, right_gram = lax.psum(
+    left_gram, right_gram = slabs_register(
         (
             jnp.dot(left_basis.T, left_basis, precision=high),
             jnp.dot(right_basis.T, right_basis, precision=high),
-        ),
-        ("blk", "plane"),
+        )
     )
     left_scale = math.sqrt(u_start.shape[0] * devices)
     right_scale = math.sqrt(v_start.shape[0] * devices)

time: 340 us -> 326 us (0.959)
  blocking collectives: 149 us -> 140 us
  waiting for transfers between devices: 141 us -> 136 us
    psum x2, blocking collectives: 117 us -> 108 us  [project_twice(): lax.psum((jnp.dot(vec, basis, precision=high), jnp.sum(vec * vec)), ('blk...]
    psum x1 -> x2, waiting for transfers between devices: 34.8 us -> 29.1 us  [the longest x1 29.1 us: _convert_stacks_all(): last = jax.lax.psum(view, along_axis)]
  transfers between devices with their start and end apart: 2 -> 3, of which waited for: 2 -> 2; matrix products, arithmetic and copies ran while one was open for 3% -> 3% of each run, Pallas kernels for 0% -> 0%
where the time goes in v2:
time: 326 us; the launch traced here: 325 us
  blocking collectives  140 us (43%)
  waiting for transfers between devices  136 us (42%)
  matrix products  19.4 us (6%)
  between operations  18.5 us (6%)
  other arithmetic  8.7 us (3%)
    psum x2, blocking collectives, project_twice(): lax.psum((jnp.dot(vec, basis, precision=high), jnp.sum(vec * vec)), ('blk...  108 us
    reduce_scatter x1, waiting for transfers between devices, on_device(): lax.psum_scatter(partial_value, ('blk', 'plane'), scatter_dimension=0, ti...  107 us
    all_gather x1, blocking collectives, on_device(): whole = lax.all_gather(rounded, ('blk', 'plane'), axis=0, tiled=True)  32 us
    psum x1, waiting for transfers between devices, _convert_stacks_all(): last = jax.lax.psum(view, along_axis)  29.1 us
  transfers between devices with their start and end apart: 3, of which 2 were waited for; matrix products, arithmetic and copies ran while one was open for 3% of the time, Pallas kernels for 0%

profile of v2, /device:TPU:12, one launch (start us, length us, event | category | flops | bytes accessed | tf_op | source)
XLA Modules:
  0.0 325.0 jit_solution(6327846638119417009)
XLA Ops:
  7.2 2.4 fusion.21
  9.6 4.0 %fusion.22 = f32[128,128]{1,0:T(8,128)} fusion(f32[2048,128]{1,0:T(8,128)} %param.15), kind=kOutput, calls=%fused_computation.48 | convolution fusion | flops 402653184 | bytes 1114112 | tf_op jit(solution)/shard_map/dot_general | solution.py:43
  13.7 1.2 compare_and_fusion
  14.9 0.8 eq.15
  15.7 0.7 compare_select_fusion
  17.0 0.7 fusion.12
  17.8 0.7 convert_element_type.14
  18.5 32.0 %all_gather.3 = bf16[65536]{0:T(1024)(128)(2,1)S(1)} all-gather(bf16[2048]{0:T(1024)(128)(2,1)S(1)} %convert_element_type.14), channel_id=1, replica_groups=mesh['blk'=8,'plane'=4] {'blk','plane'}, dimensions={0}, use_global_device_ids=true | all-gather | bytes 135168 | tf_op jit(solution)/shard_map/all_gather | solution.py:53
  50.6 1.3 gather_fusion
  51.8 0.8 select_bitcast_fusion
  52.7 1.7 fusion.8
  54.5 1.3 multiply_reduce_fusion.2
  55.8 29.1 %all-reduce.7.cloned.1.call-done = (f32[128,128]{1,0:T(8,128)}, f32[128,128]{1,0:T(8,128)}) async-done(((f32[128,128]{1,0:T(8,128)}, f32[128,128]{1,0:T(8,128)}), (f32[128,128]{1,0:T(8,128)}, f32[128,128]{1,0:T(8,128)})) %all-reduce.7.cloned.1.call-update) | async-done | bytes 131088 | tf_op jit(solution)/shard_map/psum | solution.py:10
  85.2 40.3 %all-reduce.1 = (f32[128]{0:T(128)S(1)}, f32[]{:T(128)}) all-reduce(f32[128]{0:T(128)S(1)} %convolution_bitcast_fusion.1, f32[]{:T(128)} %get-tuple-element.15), channel_id=1, replica_groups=mesh['blk'=8,'plane'=4] {'blk','plane'}, use_global_device_ids=true, to_apply=%region_1.0 | all-reduce | flops 129 | bytes 1032 | tf_op jit(solution)/shard_map/psum | solution.py:19
  125.6 1.7 multiply_reduce_fusion.4
  127.3 1.7 fusion.4
  131.8 1.2 fusion.6
  133.6 107.0 %reduce-scatter.2.cloned.1.call-done = f32[16,128]{1,0:T(8,128)} async-done(((f32[512,128]{1,0:T(8,128)}), f32[16,128]{1,0:T(8,128)}) %reduce-scatter.2.cloned.1.call-update) | async-done | bytes 8208 | tf_op jit(solution)/shard_map/reduce_scatter | solution.py:63
  240.6 1.3 multiply_reduce_fusion.1
  241.9 1.8 convolution_bitcast_fusion
  243.7 67.6 %all-reduce = (f32[128]{0:T(128)S(1)}, f32[]{:T(128)}) all-reduce(f32[128]{0:T(128)S(1)} %convolution_bitcast_fusion, f32[]{:T(128)} %get-tuple-element.11), channel_id=1, replica_groups=mesh['blk'=8,'plane'=4] {'blk','plane'}, use_global_device_ids=true, to_apply=%region_9.10 | all-reduce | flops 129 | bytes 1032 | tf_op jit(solution)/shard_map/psum | solution.py:19
  311.3 0.8 multiply_reduce_fusion.3
  312.1 0.9 fusion.5
  313.0 2.2 fusion.14
  (26 shorter events, 3.3 us)
Async XLA Ops:
  7.2 45.5 %copy-start = (bf16[4,24,128,128]{3,2,1,0:T(8,128)(2,1)S(1)}, bf16[4,24,128,128]{3,2,1,0:T(8,128)(2,1)}, u32[]{:S(2)}) copy-start(bf16[4,24,128,128]{3,2,1,0:T(8,128)(2,1)} %param.8) | copy-start | bytes 9437188
  7.2 77.8 %all-reduce.7.cloned.1.call-start = ((), (), s32[]{:S(2)}) async-start(), calls=%async_computation.2 | async-start | bytes 262144 | tf_op jit(solution)/shard_map/psum | solution.py:10
  9.6 75.4 %copy-start.1 = (f32[512,128]{1,0:T(8,128)S(1)}, f32[512,128]{1,0:T(8,128)}, u32[]{:S(2)}) copy-start(f32[512,128]{1,0:T(8,128)} %param.14) | copy-start | bytes 786436
  13.7 111.9 %all-reduce.9.cloned.1.call-start = ((), (), s32[]{:S(2)}) async-start(), calls=%async_computation.3 | async-start | bytes 262144 | tf_op jit(solution)/shard_map/psum | solution.py:11
  54.4 186.2 %copy-start.3 = (f32[2048]{0:T(1024)S(1)}, f32[2048]{0:T(1024)}, u32[]{:S(2)}) copy-start(f32[2048]{0:T(1024)} %param.12) | copy-start | bytes 24580
  85.0 155.6 %reduce-scatter.2.cloned.1.call-start = ((), (), s32[]{:S(2)}) async-start(), calls=%async_computation.1 | async-start | bytes 270336 | tf_op jit(solution)/shard_map/reduce_scatter | solution.py:63
  125.6 185.7 %copy-start.2 = (f32[128,128]{1,0:T(8,128)S(1)}, f32[128,128]{1,0:T(8,128)}, u32[]{:S(2)}) copy-start(f32[128,128]{1,0:T(8,128)} %get-tuple-element.10) | copy-start | bytes 196612
Sparse Core Ops, SparseCore 0:
  13.8 71.1 all-reduce.6
  87.3 31.5 all-reduce.8
  133.2 107.3 reduce-scatter.1
